TPU v7x, 32 devices: a whole 2x2x4 slice. The times are simulated.
32 devices in a mesh: rows: 8 (over z, x), grp: 4 (over y, core).
Axes of the slice: x: 2, y: 2, z: 4, core: 2. Of those that a mesh axis runs over, the one named last changes fastest.
Arguments:
- matrix: float32 [65536, 1024], P(('rows', 'grp'))
- row_signs: int32 [65536], P(('rows', 'grp')), may hold values from -1 to 1, as said below
- samples: int32 [8192], P(('rows', 'grp')), may hold values from 0 to 65535, as said below
Outputs:
- factor: float32 [1024, 1024], P('rows')
Inputs may be any that keep to these rules, and one draw needn't show every extreme that they name: `row_signs`: every entry is 1 or -1. `samples`: entries are distinct and increasing; entries k * 256 to (k + 1) * 256 - 1 lie in rows k * 2048 to (k + 1) * 2048 - 1.
All inputs are finite; a program needn't handle non-finite values.
Results may differ from a plain program's by a relative error of at most 0.00011.
Values sent between devices are 32-bit elements; how exact they have to be, the bound alone decides.
A program may use at most 128 MiB of HBM per device.

v0:
```python
import jax
import jax.numpy as jnp
from jax import lax
from jax.sharding import PartitionSpec as P

exact_mode = lax.Precision.HIGHEST


def parity_sign(left, right, length):
    correlation = left & right
    ones_total = jnp.zeros_like(correlation)
    for bit_level in range(max(1, length.bit_length() - 1)):
        ones_total = ones_total + (correlation >> bit_level & 1)
    return (1 - 2 * (ones_total % 2)).astype(jnp.float32)


def sylvester(length):
    indices = jnp.arange(length, dtype=jnp.int32)
    return parity_sign(indices[:, None], indices[None, :], length)


def shards(matrix, row_signs, samples):
    count_rows = lax.axis_size("rows")
    count_grp = lax.axis_size("grp")
    blocks = count_rows * count_grp
    row_dev, col_count = matrix.shape
    piece_rows = row_dev // blocks
    total_rows = row_dev * blocks
    sample_dev = samples.shape[0]
    position = lax.axis_index(("rows", "grp"))
    signed = matrix * row_signs.astype(jnp.float32)[:, None]
    before = jnp.dot(sylvester(row_dev), signed, precision=exact_mode)
    arrived = lax.all_to_all(
        lax.all_to_all(
            before.reshape(1, 1, row_dev, col_count),
            "rows",
            split_axis=2,
            concat_axis=0,
            tiled=True,
        ),
        "grp",
        split_axis=2,
        concat_axis=1,
        tiled=True,
    )
    mixed_rows = jnp.dot(
        sylvester(blocks), arrived.reshape(blocks, piece_rows * col_count), precision=exact_mode
    )
    mixed_rows = mixed_rows.reshape(count_rows, count_grp, piece_rows, col_count)
    mixed_rows = mixed_rows / jnp.sqrt(jnp.float32(total_rows))
    all_indices = lax.all_gather(samples, ("rows", "grp"), axis=0, tiled=True)
    owner_block = all_indices // row_dev
    within = all_indices % row_dev - position * piece_rows
    owner_hit = (owner_block[:, None] == jnp.arange(blocks, dtype=jnp.int32)[None, :]).astype(
        jnp.float32
    )
    local_hit = (within[:, None] == jnp.arange(piece_rows, dtype=jnp.int32)[None, :]).astype(
        jnp.float32
    )
    weights = jnp.einsum("kb,kt->bt", owner_hit, local_hit, precision=exact_mode).reshape(
        blocks * piece_rows
    )
    flat_rows = mixed_rows.reshape(blocks * piece_rows, col_count)
    local_gram = jnp.einsum(
        "kn,km->nm", flat_rows * weights[:, None], flat_rows, precision=exact_mode
    )
    summed_gram = lax.psum(local_gram, ("rows", "grp"))
    gram_total = summed_gram * (total_rows / (sample_dev * blocks))
    lower_factor = jnp.linalg.cholesky(gram_total)
    upper_factor = lower_factor.T
    share_rows = col_count // count_rows
    return lax.dynamic_slice_in_dim(
        upper_factor, lax.axis_index("rows") * share_rows, share_rows, 0
    )


def solution(mesh):
    return jax.shard_map(
        shards,
        mesh=mesh,
        in_specs=(P(("rows", "grp"), None), P(("rows", "grp")), P(("rows", "grp"))),
        out_specs=P("rows", None),
        check_vma=False,
    )
```

profile of v0, /device:TPU:0, one launch (start us, length us, event | category | flops | bytes accessed | tf_op | source)
XLA Modules:
  0.0 873.1 jit_solution(1184886997414699403)
XLA Ops:
  7.2 4.0 fusion.115
  11.2 93.9 %fusion.26 = f32[1,1,2048,1024]{3,2,1,0:T(8,128)S(1)} fusion(f32[2048,1024]{1,0:T(8,128)S(1)} %fusion.115), kind=kOutput, calls=%fused_computation.29 | convolution fusion | flops 51736739840 | bytes 16777216 | tf_op jit(solution)/shard_map/dot_general | solution.py:32
  105.2 10.7 %copy.40 = f32[1,1,2048,1024]{3,1,0,2:T(1,128)S(1)} copy(f32[1,1,2048,1024]{3,2,1,0:T(8,128)S(1)} %fusion.26) | data formatting | bytes 16777216 | tf_op jit(solution)/shard_map/reshape | solution.py:35
  115.9 190.1 %all_to_all.21 = f32[1,1,2048,1024]{3,1,0,2:T(1,128)S(1)} all-to-all(f32[1,1,2048,1024]{3,1,0,2:T(1,128)S(1)} %copy.40), channel_id=1, replica_groups=mesh['rows'=8,'grp'=4] {'rows'}, dimensions={2} | all-to-all | bytes 16777216 | tf_op jit(solution)/shard_map/all_to_all | solution.py:34
  306.0 8.1 copy.41
  314.1 5.8 all-to-all-start.1
  320.0 123.8 %all-gather = s32[32,1,256]{2,1,0:T(1,128)S(1)} all-gather(s32[1,1,256]{2,1,0:T(1,128)S(1)} %bitcast.77), channel_id=1, replica_groups=mesh['rows'=8,'grp'=4] {'rows','grp'}, dimensions={0}, use_global_device_ids=true | all-gather | bytes 33792 | tf_op jit(solution)/shard_map/all_gather | solution.py:51
  444.5 11.4 %copy.42 = f32[8,1,256,1024]{3,2,0,1:T(8,128)} copy(f32[8,1,256,1024]{3,0,1,2:T(8,128)} %all-to-all-done.1) | data formatting | bytes 16777216 | tf_op jit(solution)/shard_map/all_to_all | solution.py:33
  456.0 7.5 reshape.191
  463.4 10.6 %fusion.9 = f32[8,4,64,1024]{3,0,2,1:T(8,128)S(1)} fusion(f32[4,64,8,1024]{3,2,1,0:T(8,128)} %bitcast.73, s32[8,4]{0,1:T(4,128)S(1)} %multiply_add_fusion), kind=kOutput, calls=%fused_computation.12 | convolution fusion | flops 805336064 | bytes 16777344 | tf_op jit(solution)/shard_map/dot_general | solution.py:46
  474.1 31.2 %fusion.35 = f32[1024,1024]{0,1:T(8,128)} fusion(f32[8,4,64,1024]{3,0,2,1:T(8,128)S(1)} %fusion.9, f32[8,4,64]{0,2,1:T(8,128)S(1)} %copy.44), kind=kOutput, calls=%fused_computation.35 | convolution fusion | flops 25773998080 | bytes 12591104 | tf_op jit(solution)/shard_map/kn,km->nm/dot_general | solution.py:64
  505.4 138.7 %all-reduce.3.cloned.1.call-done = f32[1024,1024]{0,1:T(8,128)} async-done(((f32[1024,1024]{0,1:T(8,128)}), f32[1024,1024]{0,1:T(8,128)}) %all-reduce.3.cloned.1.call-update) | async-done | bytes 4194320 | tf_op jit(solution)/shard_map/psum | solution.py:67
  644.0 5.0 broadcast_multiply_fusion
  649.0 5.3 copy.46
  654.4 4.4 fusion.31
  658.8 1.9 copy-done
  660.8 11.7 %cholesky.223 = f32[128,128]{1,0:T(8,128)S(1)} custom-call(f32[128,128]{1,0:T(8,128)S(1)} %cholesky.580), custom_call_target="Cholesky" | custom-call | tf_op jit(solution)/shard_map/jit(cholesky)/cholesky | solution.py:69
  672.5 2.5 cholesky.255
  675.0 9.8 %custom-call.59 = f32[1,128,128]{1,2,0:T(8,128)S(1)} custom-call(f32[1,128,128]{2,1,0:T(8,128)S(1)} %get-tuple-element.26), custom_call_target="InvertDiagBlocksLowerTriangular" | custom-call | tf_op jit(solution)/shard_map/jit(cholesky)/cholesky | solution.py:69
  684.8 2.4 constant_dynamic-update-slice_fusion.7
  687.2 1.5 convolution_subtract_fusion
  688.8 12.1 %cholesky.244 = f32[128,128]{1,0:T(8,128)S(1)} custom-call(f32[128,128]{1,0:T(8,128)S(1)} %cholesky.584), custom_call_target="Cholesky" | custom-call | tf_op jit(solution)/shard_map/jit(cholesky)/cholesky | solution.py:69
  701.5 9.8 %custom-call.60 = f32[1,128,128]{1,2,0:T(8,128)S(1)} custom-call(f32[1,128,128]{2,1,0:T(8,128)S(1)} %get-tuple-element.23), custom_call_target="InvertDiagBlocksLowerTriangular" | custom-call | tf_op jit(solution)/shard_map/jit(cholesky)/cholesky | solution.py:69
  711.3 1.2 convolution_dynamic-update-slice_fusion
  712.6 2.1 convolution_subtract_fusion.1
  714.7 11.7 %cholesky.468 = f32[128,128]{1,0:T(8,128)S(1)} custom-call(f32[128,128]{1,0:T(8,128)S(1)} %cholesky.589), custom_call_target="Cholesky" | custom-call | tf_op jit(solution)/shard_map/jit(cholesky)/cholesky | solution.py:69
  727.0 9.8 %custom-call.61 = f32[1,128,128]{1,2,0:T(8,128)S(1)} custom-call(f32[1,128,128]{2,1,0:T(8,128)S(1)} %get-tuple-element.20), custom_call_target="InvertDiagBlocksLowerTriangular" | custom-call | tf_op jit(solution)/shard_map/jit(cholesky)/cholesky | solution.py:69
  736.8 1.2 convolution_dynamic-update-slice_fusion.1
  738.0 2.3 convolution_subtract_fusion.2
  740.3 11.9 %cholesky.487 = f32[128,128]{1,0:T(8,128)S(1)} custom-call(f32[128,128]{1,0:T(8,128)S(1)} %cholesky.594), custom_call_target="Cholesky" | custom-call | tf_op jit(solution)/shard_map/jit(cholesky)/cholesky | solution.py:69
  752.9 9.8 %custom-call.62 = f32[1,128,128]{1,2,0:T(8,128)S(1)} custom-call(f32[1,128,128]{2,1,0:T(8,128)S(1)} %get-tuple-element.17), custom_call_target="InvertDiagBlocksLowerTriangular" | custom-call | tf_op jit(solution)/shard_map/jit(cholesky)/cholesky | solution.py:69
  762.7 1.1 convolution_dynamic-update-slice_fusion.2
  763.8 2.3 convolution_subtract_fusion.3
  766.1 11.7 %cholesky.506 = f32[128,128]{1,0:T(8,128)S(1)} custom-call(f32[128,128]{1,0:T(8,128)S(1)} %cholesky.599), custom_call_target="Cholesky" | custom-call | tf_op jit(solution)/shard_map/jit(cholesky)/cholesky | solution.py:69
  778.5 10.0 %custom-call.63 = f32[1,128,128]{1,2,0:T(8,128)S(1)} custom-call(f32[1,128,128]{2,1,0:T(8,128)S(1)} %get-tuple-element.14), custom_call_target="InvertDiagBlocksLowerTriangular" | custom-call | tf_op jit(solution)/shard_map/jit(cholesky)/cholesky | solution.py:69
  788.5 1.0 convolution_dynamic-update-slice_fusion.3
  789.5 2.3 convolution_subtract_fusion.4
  791.8 11.7 %cholesky.526 = f32[128,128]{1,0:T(8,128)S(1)} custom-call(f32[128,128]{1,0:T(8,128)S(1)} %cholesky.604), custom_call_target="Cholesky" | custom-call | tf_op jit(solution)/shard_map/jit(cholesky)/cholesky | solution.py:69
  804.2 9.8 %custom-call.64 = f32[1,128,128]{1,2,0:T(8,128)S(1)} custom-call(f32[1,128,128]{2,1,0:T(8,128)S(1)} %get-tuple-element.11), custom_call_target="InvertDiagBlocksLowerTriangular" | custom-call | tf_op jit(solution)/shard_map/jit(cholesky)/cholesky | solution.py:69
  814.0 0.9 convolution_dynamic-update-slice_fusion.4
  814.9 2.0 convolution_subtract_fusion.5
  817.0 11.7 %cholesky.546 = f32[128,128]{1,0:T(8,128)S(1)} custom-call(f32[128,128]{1,0:T(8,128)S(1)} %cholesky.609), custom_call_target="Cholesky" | custom-call | tf_op jit(solution)/shard_map/jit(cholesky)/cholesky | solution.py:69
  829.3 9.8 %custom-call.65 = f32[1,128,128]{1,2,0:T(8,128)S(1)} custom-call(f32[1,128,128]{2,1,0:T(8,128)S(1)} %get-tuple-element.8), custom_call_target="InvertDiagBlocksLowerTriangular" | custom-call | tf_op jit(solution)/shard_map/jit(cholesky)/cholesky | solution.py:69
  839.2 0.8 convolution_dynamic-update-slice_fusion.5
  840.0 1.8 convolution_subtract_fusion.6
  841.8 11.7 %cholesky.564 = f32[128,128]{1,0:T(8,128)S(1)} custom-call(f32[128,128]{1,0:T(8,128)S(1)} %convolution_subtract_fusion.6), custom_call_target="Cholesky" | custom-call | tf_op jit(solution)/shard_map/jit(cholesky)/cholesky | solution.py:69
  863.7 1.1 fusion.49
  864.8 1.0 copy.47
  (33 shorter events, 10.7 us)
Async XLA Ops:
  314.1 5.9 copy-start.1
  314.1 130.4 %all-to-all-start.1 = ((f32[8,1,256,1024]{3,0,1,2:T(8,128)}), f32[8,1,256,1024]{3,0,1,2:T(8,128)}, u32[]{:S(2)}, u32[]{:S(2)}) async-start(f32[8,1,256,1024]{3,0,1,2:T(8,128)} %copy.41), calls=%async_computation.1 | async-start | bytes 16777216 | tf_op jit(solution)/shard_map/all_to_all | solution.py:33
  319.9 324.1 %all-reduce.3.cloned.1.call-start = ((), (), s32[]{:S(2)}) async-start(), calls=%async_computation.2 | async-start | bytes 8388608 | tf_op jit(solution)/shard_map/psum | solution.py:67
  658.8 1.9 copy-start
Sparse Core Ops, SparseCore 0:
  505.5 138.4 all-reduce.2
where the time goes:
time: 885 us; the launch traced here: 873 us
  blocking collectives  314 us (35%)
  other arithmetic  188 us (21%)
  matrix products  159 us (18%)
  waiting for transfers between devices  139 us (16%)
  local copies, waits for them, and re-layouts  48.6 us (5%)
  between operations  19.1 us (2%)
    all_to_all x1, blocking collectives, shards(): lax.all_to_all(before.reshape(1, 1, row_dev, col_count), 'rows', split_ax...  190 us
    another operation x30, other arithmetic, shards(): lower_factor = jnp.linalg.cholesky(gram_total)  172 us
    psum x1, waiting for transfers between devices, shards(): summed_gram = lax.psum(local_gram, ('rows', 'grp'))  139 us
    all_gather x1, blocking collectives, shards(): all_indices = lax.all_gather(samples, ('rows', 'grp'), axis=0, tiled=True)  124 us
    dot_general x1, matrix products, shards(): before = jnp.dot(sylvester(row_dev), signed, precision=exact_mode)  93.9 us
    dot_general x1, matrix products, shards(): jnp.einsum('kn,km->nm', flat_rows * weights[:, None], flat_rows, precisio...  31.2 us
    another operation x14, matrix products, shards(): lower_factor = jnp.linalg.cholesky(gram_total)  23.1 us
  transfers between devices with their start and end apart: 2, of which 1 were waited for; matrix products, arithmetic and copies ran while one was open for 0% of the time, Pallas kernels for 0%

commit v1 on v0

--- a/solution.py
+++ b/solution.py
@@ -64,7 +64,8 @@
     local_gram = jnp.einsum(
         "kn,km->nm", flat_rows * weights[:, None], flat_rows, precision=exact_mode
     )
-    summed_gram = lax.psum(local_gram, ("rows", "grp"))
+    one_axis = lax.psum(local_gram, "grp")
+    summed_gram = lax.psum(one_axis, "rows")
     gram_total = summed_gram * (total_rows / (sample_dev * blocks))
     lower_factor = jnp.linalg.cholesky(gram_total)
     upper_factor = lower_factor.T

time: 885 us -> 988 us (1.12)
  waiting for transfers between devices: 139 us -> 242 us
    psum x1 -> x2, waiting for transfers between devices: 139 us -> 242 us  [the longest x1 160 us: shards(): summed_gram = lax.psum(one_axis, 'rows')]
  transfers between devices with their start and end apart: 2 -> 3, of which waited for: 1 -> 2; matrix products, arithmetic and copies ran while one was open for 0% -> 0% of each run, Pallas kernels for 0% -> 0%
where the time goes in v1:
time: 988 us; the launch traced here: 976 us
  blocking collectives  314 us (32%)
  waiting for transfers between devices  242 us (24%)
  other arithmetic  188 us (19%)
  matrix products  159 us (16%)
  local copies, waits for them, and re-layouts  48.6 us (5%)
  between operations  19.1 us (2%)
    all_to_all x1, blocking collectives, shards(): lax.all_to_all(before.reshape(1, 1, row_dev, col_count), 'rows', split_ax...  190 us
    another operation x30, other arithmetic, shards(): lower_factor = jnp.linalg.cholesky(gram_total)  172 us
    psum x1, waiting for transfers between devices, shards(): summed_gram = lax.psum(one_axis, 'rows')  160 us
    all_gather x1, blocking collectives, shards(): all_indices = lax.all_gather(samples, ('rows', 'grp'), axis=0, tiled=True)  124 us
    dot_general x1, matrix products, shards(): before = jnp.dot(sylvester(row_dev), signed, precision=exact_mode)  93.9 us
    psum x1, waiting for transfers between devices, shards(): one_axis = lax.psum(local_gram, 'grp')  81.7 us
    dot_general x1, matrix products, shards(): jnp.einsum('kn,km->nm', flat_rows * weights[:, None], flat_rows, precisio...  31.2 us
    another operation x14, matrix products, shards(): lower_factor = jnp.linalg.cholesky(gram_total)  23.1 us
  transfers between devices with their start and end apart: 3, of which 2 were waited for; matrix products, arithmetic and copies ran while one was open for 0% of the time, Pallas kernels for 0%

profile of v1, /device:TPU:0, one launch (start us, length us, event | category | flops | bytes accessed | tf_op | source)
XLA Modules:
  0.0 976.4 jit_solution(3706182834538380781)
XLA Ops:
  7.2 4.0 fusion.115
  11.2 93.9 %fusion.26 = f32[1,1,2048,1024]{3,2,1,0:T(8,128)S(1)} fusion(f32[2048,1024]{1,0:T(8,128)S(1)} %fusion.115), kind=kOutput, calls=%fused_computation.29 | convolution fusion | flops 51736739840 | bytes 16777216 | tf_op jit(solution)/shard_map/dot_general | solution.py:32
  105.2 10.7 %copy.40 = f32[1,1,2048,1024]{3,1,0,2:T(1,128)S(1)} copy(f32[1,1,2048,1024]{3,2,1,0:T(8,128)S(1)} %fusion.26) | data formatting | bytes 16777216 | tf_op jit(solution)/shard_map/reshape | solution.py:35
  115.9 190.1 %all_to_all.21 = f32[1,1,2048,1024]{3,1,0,2:T(1,128)S(1)} all-to-all(f32[1,1,2048,1024]{3,1,0,2:T(1,128)S(1)} %copy.40), channel_id=1, replica_groups=mesh['rows'=8,'grp'=4] {'rows'}, dimensions={2} | all-to-all | bytes 16777216 | tf_op jit(solution)/shard_map/all_to_all | solution.py:34
  306.0 8.1 copy.41
  314.1 5.8 all-to-all-start.1
  320.0 123.8 %all-gather = s32[32,1,256]{2,1,0:T(1,128)S(1)} all-gather(s32[1,1,256]{2,1,0:T(1,128)S(1)} %bitcast.77), channel_id=1, replica_groups=mesh['rows'=8,'grp'=4] {'rows','grp'}, dimensions={0}, use_global_device_ids=true | all-gather | bytes 33792 | tf_op jit(solution)/shard_map/all_gather | solution.py:51
  444.5 11.4 %copy.42 = f32[8,1,256,1024]{3,2,0,1:T(8,128)} copy(f32[8,1,256,1024]{3,0,1,2:T(8,128)} %all-to-all-done.1) | data formatting | bytes 16777216 | tf_op jit(solution)/shard_map/all_to_all | solution.py:33
  456.0 7.5 reshape.191
  463.4 10.6 %fusion.9 = f32[8,4,64,1024]{3,0,2,1:T(8,128)S(1)} fusion(f32[4,64,8,1024]{3,2,1,0:T(8,128)} %bitcast.73, s32[8,4]{0,1:T(4,128)S(1)} %multiply_add_fusion), kind=kOutput, calls=%fused_computation.12 | convolution fusion | flops 805336064 | bytes 16777344 | tf_op jit(solution)/shard_map/dot_general | solution.py:46
  474.1 31.2 %fusion.35 = f32[1024,1024]{0,1:T(8,128)} fusion(f32[8,4,64,1024]{3,0,2,1:T(8,128)S(1)} %fusion.9, f32[8,4,64]{0,2,1:T(8,128)S(1)} %copy.44), kind=kOutput, calls=%fused_computation.35 | convolution fusion | flops 25773998080 | bytes 12591104 | tf_op jit(solution)/shard_map/kn,km->nm/dot_general | solution.py:64
  505.3 81.7 %all-reduce.4.cloned.1.call-done = f32[1024,1024]{0,1:T(8,128)} async-done(((f32[1024,1024]{0,1:T(8,128)}), f32[1024,1024]{0,1:T(8,128)}) %all-reduce.4.cloned.1.call-update) | async-done | bytes 4194320 | tf_op jit(solution)/shard_map/psum | solution.py:67
  587.1 160.2 %all-reduce.6.cloned.1.call-done = f32[1024,1024]{0,1:T(8,128)} async-done(((f32[1024,1024]{0,1:T(8,128)}), f32[1024,1024]{0,1:T(8,128)}) %all-reduce.6.cloned.1.call-update) | async-done | bytes 4194320 | tf_op jit(solution)/shard_map/psum | solution.py:68
  747.3 5.0 broadcast_multiply_fusion
  752.3 5.3 copy.46
  757.7 4.4 fusion.31
  762.1 1.9 copy-done
  764.1 11.7 %cholesky.223 = f32[128,128]{1,0:T(8,128)S(1)} custom-call(f32[128,128]{1,0:T(8,128)S(1)} %cholesky.580), custom_call_target="Cholesky" | custom-call | tf_op jit(solution)/shard_map/jit(cholesky)/cholesky | solution.py:70
  775.8 2.5 cholesky.255
  778.3 9.8 %custom-call.59 = f32[1,128,128]{1,2,0:T(8,128)S(1)} custom-call(f32[1,128,128]{2,1,0:T(8,128)S(1)} %get-tuple-element.26), custom_call_target="InvertDiagBlocksLowerTriangular" | custom-call | tf_op jit(solution)/shard_map/jit(cholesky)/cholesky | solution.py:70
  788.1 2.4 constant_dynamic-update-slice_fusion.7
  790.5 1.5 convolution_subtract_fusion
  792.1 12.1 %cholesky.244 = f32[128,128]{1,0:T(8,128)S(1)} custom-call(f32[128,128]{1,0:T(8,128)S(1)} %cholesky.584), custom_call_target="Cholesky" | custom-call | tf_op jit(solution)/shard_map/jit(cholesky)/cholesky | solution.py:70
  804.8 9.8 %custom-call.60 = f32[1,128,128]{1,2,0:T(8,128)S(1)} custom-call(f32[1,128,128]{2,1,0:T(8,128)S(1)} %get-tuple-element.23), custom_call_target="InvertDiagBlocksLowerTriangular" | custom-call | tf_op jit(solution)/shard_map/jit(cholesky)/cholesky | solution.py:70
  814.6 1.2 convolution_dynamic-update-slice_fusion
  815.9 2.1 convolution_subtract_fusion.1
  818.0 11.7 %cholesky.468 = f32[128,128]{1,0:T(8,128)S(1)} custom-call(f32[128,128]{1,0:T(8,128)S(1)} %cholesky.589), custom_call_target="Cholesky" | custom-call | tf_op jit(solution)/shard_map/jit(cholesky)/cholesky | solution.py:70
  830.3 9.8 %custom-call.61 = f32[1,128,128]{1,2,0:T(8,128)S(1)} custom-call(f32[1,128,128]{2,1,0:T(8,128)S(1)} %get-tuple-element.20), custom_call_target="InvertDiagBlocksLowerTriangular" | custom-call | tf_op jit(solution)/shard_map/jit(cholesky)/cholesky | solution.py:70
  840.1 1.2 convolution_dynamic-update-slice_fusion.1
  841.3 2.3 convolution_subtract_fusion.2
  843.7 11.9 %cholesky.487 = f32[128,128]{1,0:T(8,128)S(1)} custom-call(f32[128,128]{1,0:T(8,128)S(1)} %cholesky.594), custom_call_target="Cholesky" | custom-call | tf_op jit(solution)/shard_map/jit(cholesky)/cholesky | solution.py:70
  856.2 9.8 %custom-call.62 = f32[1,128,128]{1,2,0:T(8,128)S(1)} custom-call(f32[1,128,128]{2,1,0:T(8,128)S(1)} %get-tuple-element.17), custom_call_target="InvertDiagBlocksLowerTriangular" | custom-call | tf_op jit(solution)/shard_map/jit(cholesky)/cholesky | solution.py:70
  866.0 1.1 convolution_dynamic-update-slice_fusion.2
  867.1 2.3 convolution_subtract_fusion.3
  869.5 11.7 %cholesky.506 = f32[128,128]{1,0:T(8,128)S(1)} custom-call(f32[128,128]{1,0:T(8,128)S(1)} %cholesky.599), custom_call_target="Cholesky" | custom-call | tf_op jit(solution)/shard_map/jit(cholesky)/cholesky | solution.py:70
  881.8 10.0 %custom-call.63 = f32[1,128,128]{1,2,0:T(8,128)S(1)} custom-call(f32[1,128,128]{2,1,0:T(8,128)S(1)} %get-tuple-element.14), custom_call_target="InvertDiagBlocksLowerTriangular" | custom-call | tf_op jit(solution)/shard_map/jit(cholesky)/cholesky | solution.py:70
  891.8 1.0 convolution_dynamic-update-slice_fusion.3
  892.9 2.3 convolution_subtract_fusion.4
  895.2 11.7 %cholesky.526 = f32[128,128]{1,0:T(8,128)S(1)} custom-call(f32[128,128]{1,0:T(8,128)S(1)} %cholesky.604), custom_call_target="Cholesky" | custom-call | tf_op jit(solution)/shard_map/jit(cholesky)/cholesky | solution.py:70
  907.5 9.8 %custom-call.64 = f32[1,128,128]{1,2,0:T(8,128)S(1)} custom-call(f32[1,128,128]{2,1,0:T(8,128)S(1)} %get-tuple-element.11), custom_call_target="InvertDiagBlocksLowerTriangular" | custom-call | tf_op jit(solution)/shard_map/jit(cholesky)/cholesky | solution.py:70
  917.3 0.9 convolution_dynamic-update-slice_fusion.4
  918.2 2.0 convolution_subtract_fusion.5
  920.3 11.7 %cholesky.546 = f32[128,128]{1,0:T(8,128)S(1)} custom-call(f32[128,128]{1,0:T(8,128)S(1)} %cholesky.609), custom_call_target="Cholesky" | custom-call | tf_op jit(solution)/shard_map/jit(cholesky)/cholesky | solution.py:70
  932.7 9.8 %custom-call.65 = f32[1,128,128]{1,2,0:T(8,128)S(1)} custom-call(f32[1,128,128]{2,1,0:T(8,128)S(1)} %get-tuple-element.8), custom_call_target="InvertDiagBlocksLowerTriangular" | custom-call | tf_op jit(solution)/shard_map/jit(cholesky)/cholesky | solution.py:70
  943.3 1.8 convolution_subtract_fusion.6
  945.1 11.7 %cholesky.564 = f32[128,128]{1,0:T(8,128)S(1)} custom-call(f32[128,128]{1,0:T(8,128)S(1)} %convolution_subtract_fusion.6), custom_call_target="Cholesky" | custom-call | tf_op jit(solution)/shard_map/jit(cholesky)/cholesky | solution.py:70
  967.0 1.1 fusion.49
  968.2 1.0 copy.47
  (36 shorter events, 11.6 us)
Async XLA Ops:
  314.1 5.9 copy-start.1
  314.1 130.4 %all-to-all-start.1 = ((f32[8,1,256,1024]{3,0,1,2:T(8,128)}), f32[8,1,256,1024]{3,0,1,2:T(8,128)}, u32[]{:S(2)}, u32[]{:S(2)}) async-start(f32[8,1,256,1024]{3,0,1,2:T(8,128)} %copy.41), calls=%async_computation.1 | async-start | bytes 16777216 | tf_op jit(solution)/shard_map/all_to_all | solution.py:33
  319.9 267.2 %all-reduce.4.cloned.1.call-start = ((), (), s32[]{:S(2)}) async-start(), calls=%async_computation.2 | async-start | bytes 8388608 | tf_op jit(solution)/shard_map/psum | solution.py:67
  505.3 242.0 %all-reduce.6.cloned.1.call-start = ((), (), s32[]{:S(2)}) async-start(), calls=%async_computation.3 | async-start | bytes 8388608 | tf_op jit(solution)/shard_map/psum | solution.py:68
  762.1 1.9 copy-start
Sparse Core Ops, SparseCore 0:
  505.4 81.5 all-reduce.3
  590.7 156.5 all-reduce.5
